TPU v7x, 32 devices: a whole 2x2x4 slice. The times are simulated.
32 devices in a mesh: dp: 8 (over z, x), tensor: 4 (over y, core).
Axes of the slice: x: 2, y: 2, z: 4, core: 2. Of those that a mesh axis runs over, the one named last changes fastest.
Arguments:
- inputs: bfloat16 [8, 64, 64, 1280], P('dp', 'tensor'), may hold values from -6 to 6
- cotangent: bfloat16 [8, 64, 64, 1280], P('dp', 'tensor'), may hold values from -6 to 6
- teacher: bfloat16 [8, 64, 64, 1280], P('dp', 'tensor'), may hold values from -6 to 6
- qkv_weight: bfloat16 [3, 1280, 1280], P(None, 'dp', 'tensor'), may hold values from -0.15625 to 0.15625
- proj_weight: bfloat16 [1280, 1280], P('tensor', 'dp'), may hold values from -1 to 1
- up_weight: bfloat16 [1280, 5120], P('dp', 'tensor'), may hold values from -0.15625 to 0.15625
- down_weight: bfloat16 [5120, 1280], P('tensor', 'dp'), may hold values from -0.078125 to 0.078125
- qv_bias: bfloat16 [2, 1280], P(None, 'tensor'), may hold values from -3 to 3
- up_bias: bfloat16 [5120], P('tensor'), may hold values from -3 to 3
- norm_gains: bfloat16 [2, 1280], replicated, may hold values from 0.5 to 1.5
- norm_shifts: bfloat16 [2, 1280], replicated, may hold values from -3 to 3
- out_biases: bfloat16 [2, 1280], replicated, may hold values from -3 to 3
- rel_tables: bfloat16 [2, 27, 80], replicated, may hold values from -0.625 to 0.625
Outputs:
- output: bfloat16 [8, 64, 64, 1280], P('dp', 'tensor')
- input_grad: float32 [8, 64, 64, 1280], P('dp', 'tensor')
- loss: float32 [], replicated
- qkv_weight_grad: float32 [3, 1280, 1280], P(None, 'dp', 'tensor')
- proj_weight_grad: float32 [1280, 1280], P('tensor', 'dp')
- up_weight_grad: float32 [1280, 5120], P('dp', 'tensor')
- down_weight_grad: float32 [5120, 1280], P('tensor', 'dp')
- qv_bias_grad: float32 [2, 1280], P(None, 'tensor')
- up_bias_grad: float32 [5120], P('tensor')
- norm_gains_grad: float32 [2, 1280], replicated
- norm_shifts_grad: float32 [2, 1280], replicated
- out_biases_grad: float32 [2, 1280], replicated
- rel_tables_grad: float32 [2, 27, 80], replicated
All inputs are finite; a program needn't handle non-finite values.
Results may differ from a plain program's by a relative error of at most 0.013.
Values may be sent and summed in bfloat16 or wider, within the bound.
A program may use at most 256 MiB of HBM per device.

v0:
```python
from functools import partial
import jax
import jax.numpy as jnp
from jax import lax
from jax.sharding import PartitionSpec as P

D = 1280
HEAD_DIM = 80
GRID = 64
WIN = 14
PGRID = 70
NWIN = 5
highest = lax.Precision.HIGHEST


def layer_norm(values, gain_vector, shift_vector):
    average = jnp.mean(values, axis=-1, keepdims=True)
    centred = values - average
    variance = jnp.mean(centred * centred, axis=-1, keepdims=True)
    return centred * lax.rsqrt(variance + 1e-06) * gain_vector + shift_vector


def exact_gelu(values):
    return jax.nn.gelu(values, approximate=False)


def offset_tables(window):
    position = jnp.arange(window * window)
    across = jnp.arange(window)
    ranks = jnp.arange(2 * window - 1)
    high_sel = (
        position[:, None, None] // window - across[None, :, None] + window - 1
        == ranks[None, None, :]
    ).astype(jnp.float32)
    wide_sel = (
        position[:, None, None] % window - across[None, :, None] + window - 1
        == ranks[None, None, :]
    ).astype(jnp.float32)
    return (high_sel, wide_sel)


def to_windows(grid_values):
    extra = PGRID - GRID
    padded = jnp.pad(grid_values, ((0, extra), (0, extra), (0, 0)))
    channels = grid_values.shape[-1]
    shaped = padded.reshape(NWIN, WIN, NWIN, WIN, channels).transpose(0, 2, 1, 3, 4)
    return shaped.reshape(NWIN, NWIN, WIN * WIN, channels)


def from_windows(windowed):
    channels = windowed.shape[-1]
    shaped = windowed.reshape(NWIN, NWIN, WIN, WIN, channels).transpose(0, 2, 1, 3, 4)
    return shaped.reshape(PGRID, PGRID, channels)[:GRID, :GRID]


def score_block(queries, key_rows, tables, selectors):
    table_high, table_wide = tables
    high_sel, wide_sel = selectors
    raw = jnp.einsum(
        "wqhc,wkhc->whqk", queries, key_rows, preferred_element_type=jnp.float32
    ) * HEAD_DIM ** (-0.5)
    along_high = jnp.einsum(
        "wqhc,rc->wqhr", queries, table_high, preferred_element_type=jnp.float32
    )
    along_wide = jnp.einsum(
        "wqhc,rc->wqhr", queries, table_wide, preferred_element_type=jnp.float32
    )
    bias_high = jnp.einsum("wqhr,qkr->whqk", along_high, high_sel, precision=highest)
    bias_wide = jnp.einsum("wqhr,qkr->whqk", along_wide, wide_sel, precision=highest)
    shaped = (
        raw.reshape(raw.shape[:3] + (WIN, WIN)) + bias_high[..., :, None] + bias_wide[..., None, :]
    )
    return shaped.reshape(raw.shape)


def attend_row(block_parts, tables, selectors):
    queries, key_rows, value_rows = block_parts
    scores = score_block(queries, key_rows, tables, selectors)
    row_max = jnp.max(scores, axis=-1, keepdims=True)
    shifted = jnp.exp(scores - row_max)
    row_total = jnp.sum(shifted, axis=-1, keepdims=True)
    probs_low = (shifted / row_total).astype(jnp.bfloat16)
    attended = jnp.einsum(
        "whqk,wkhc->wqhc", probs_low, value_rows, preferred_element_type=jnp.float32
    )
    return (attended.astype(jnp.bfloat16), (row_max + jnp.log(row_total))[..., 0])


def attend_back(block_parts, tables, selectors):
    queries, key_rows, value_rows, attended_grad, log_total = block_parts
    high_sel, wide_sel = selectors
    scores = score_block(queries, key_rows, tables, selectors)
    probs = jnp.exp(scores - log_total[..., None])
    probs_grad = jnp.einsum(
        "wqhc,wkhc->whqk", attended_grad, value_rows, preferred_element_type=jnp.float32
    )
    value_grad = jnp.einsum(
        "whqk,wqhc->wkhc",
        probs.astype(jnp.bfloat16),
        attended_grad,
        preferred_element_type=jnp.float32,
    )
    scores_grad = probs * (probs_grad - jnp.sum(probs * probs_grad, axis=-1, keepdims=True))
    scores_low = scores_grad.astype(jnp.bfloat16)
    query_grad = jnp.einsum(
        "whqk,wkhc->wqhc", scores_low, key_rows, preferred_element_type=jnp.float32
    ) * HEAD_DIM ** (-0.5)
    key_grad = jnp.einsum(
        "whqk,wqhc->wkhc", scores_low, queries, preferred_element_type=jnp.float32
    ) * HEAD_DIM ** (-0.5)
    shaped = scores_grad.reshape(scores_grad.shape[:3] + (WIN, WIN))
    rank_high = jnp.einsum("whqa,qar->wqhr", jnp.sum(shaped, axis=-1), high_sel, precision=highest)
    rank_wide = jnp.einsum("whqb,qbr->wqhr", jnp.sum(shaped, axis=-2), wide_sel, precision=highest)
    table_high = tables[0].astype(jnp.float32)
    table_wide = tables[1].astype(jnp.float32)
    query_grad = query_grad + jnp.einsum("wqhr,rc->wqhc", rank_high, table_high, precision=highest)
    query_grad = query_grad + jnp.einsum("wqhr,rc->wqhc", rank_wide, table_wide, precision=highest)
    query_wide = queries.astype(jnp.float32)
    table_grad = jnp.stack(
        [
            jnp.einsum("wqhr,wqhc->rc", rank_high, query_wide, precision=highest),
            jnp.einsum("wqhr,wqhc->rc", rank_wide, query_wide, precision=highest),
        ]
    )
    return (query_grad, key_grad, value_grad, table_grad)


def shards(
    inputs,
    cotangent,
    teacher,
    qkv_weight,
    proj_weight,
    up_weight,
    down_weight,
    qv_bias,
    up_bias,
    norm_gains,
    norm_shifts,
    out_biases,
    rel_tables,
):
    qkv_full, proj_full, up_full, down_full = (
        lax.all_gather(qkv_weight, "dp", axis=1, tiled=True),
        lax.all_gather(proj_weight, "dp", axis=1, tiled=True),
        lax.all_gather(up_weight, "dp", axis=0, tiled=True),
        lax.all_gather(down_weight, "dp", axis=1, tiled=True),
    )
    up_matrix, down_matrix, up_bias_all = (up_full, down_full, up_bias)
    images, row_count = (inputs.shape[0], inputs.shape[1])
    local_width = qkv_full.shape[2]
    head_count = local_width // HEAD_DIM
    head_shape = (NWIN, NWIN, WIN * WIN, head_count, HEAD_DIM)
    selectors = offset_tables(WIN)
    tables = (rel_tables[0], rel_tables[1])
    gains_wide = norm_gains.astype(jnp.float32)
    shifts_wide = norm_shifts.astype(jnp.float32)
    source = inputs[0].astype(jnp.float32)
    normed = layer_norm(source, gains_wide[0], shifts_wide[0]).astype(jnp.bfloat16)
    gathered = lax.all_gather(normed, "tensor", axis=0, tiled=True)
    windows = to_windows(gathered)
    projected = jnp.einsum("abpd,sdc->sabpc", windows, qkv_full, preferred_element_type=jnp.float32)
    queries = (projected[0] + qv_bias[0]).astype(jnp.bfloat16).reshape(head_shape)
    key_rows = projected[1].astype(jnp.bfloat16).reshape(head_shape)
    value_rows = (projected[2] + qv_bias[1]).astype(jnp.bfloat16).reshape(head_shape)
    attended, log_totals = lax.map(
        partial(attend_row, tables=tables, selectors=selectors), (queries, key_rows, value_rows)
    )
    grid_out = from_windows(attended.reshape(NWIN, NWIN, WIN * WIN, local_width))
    row_piece = grid_out
    attn_branch = lax.psum_scatter(
        jnp.einsum("xyc,cd->xyd", row_piece, proj_full, preferred_element_type=jnp.float32).astype(
            jnp.bfloat16
        ),
        "tensor",
        scatter_dimension=0,
        tiled=True,
    ).astype(jnp.float32)
    middle = source + attn_branch + out_biases[0].astype(jnp.float32)
    normed_two = layer_norm(middle, gains_wide[1], shifts_wide[1]).astype(jnp.bfloat16)
    mlp_input = lax.all_gather(normed_two, "tensor", axis=0, tiled=True)
    hidden = (
        jnp.einsum("xyd,dm->xym", mlp_input, up_matrix, preferred_element_type=jnp.float32)
        + up_bias_all
    )
    active = exact_gelu(hidden).astype(jnp.bfloat16)
    row_piece = active
    mlp_branch = lax.psum_scatter(
        jnp.einsum(
            "xym,md->xyd", row_piece, down_matrix, preferred_element_type=jnp.float32
        ).astype(jnp.bfloat16),
        "tensor",
        scatter_dimension=0,
        tiled=True,
    ).astype(jnp.float32)
    result = middle + mlp_branch + out_biases[1].astype(jnp.float32)
    mismatch = result - teacher[0].astype(jnp.float32)
    loss_total = jnp.sum(mismatch * mismatch)
    outputs = [result.astype(jnp.bfloat16)]
    result_grad = cotangent[0].astype(jnp.float32) + mismatch
    result_low = result_grad.astype(jnp.bfloat16)
    grad_rows = lax.all_gather(result_low, "tensor", axis=0, tiled=True)
    down_acc = jnp.einsum("xym,xyd->md", active, grad_rows, preferred_element_type=jnp.float32)
    active_grad = jnp.einsum(
        "xyd,md->xym", grad_rows, down_matrix, preferred_element_type=jnp.float32
    )
    gelu_value, gelu_back = jax.vjp(exact_gelu, hidden)
    hidden_grad = gelu_back(active_grad)[0]
    up_bias_acc = jnp.sum(hidden_grad, axis=(0, 1))
    hidden_low = hidden_grad.astype(jnp.bfloat16)
    up_acc = jnp.einsum("xyd,xym->dm", mlp_input, hidden_low, preferred_element_type=jnp.float32)
    row_piece = hidden_low
    second_grad = lax.psum_scatter(
        jnp.einsum("xym,dm->xyd", row_piece, up_matrix, preferred_element_type=jnp.float32).astype(
            jnp.bfloat16
        ),
        "tensor",
        scatter_dimension=0,
        tiled=True,
    ).astype(jnp.float32)
    second_value, second_back = jax.vjp(layer_norm, middle, gains_wide[1], shifts_wide[1])
    middle_part, second_gain, second_shift = second_back(second_grad)
    middle_grad = result_grad + middle_part
    out_bias_acc = jnp.stack([jnp.sum(middle_grad, axis=(0, 1)), jnp.sum(result_grad, axis=(0, 1))])
    middle_low = middle_grad.astype(jnp.bfloat16)
    gathered_grad = lax.all_gather(middle_low, "tensor", axis=0, tiled=True)
    proj_acc = jnp.einsum(
        "xyc,xyd->cd", grid_out, gathered_grad, preferred_element_type=jnp.float32
    )
    attended_grad = jnp.einsum(
        "xyd,cd->xyc", gathered_grad, proj_full, preferred_element_type=jnp.float32
    ).astype(jnp.bfloat16)
    grad_windows = to_windows(attended_grad).reshape(head_shape)
    query_grad, key_grad, value_grad, table_parts = lax.map(
        partial(attend_back, tables=tables, selectors=selectors),
        (queries, key_rows, value_rows, grad_windows, log_totals),
    )
    table_acc = jnp.sum(table_parts, axis=0)
    query_flat = query_grad.reshape(NWIN, NWIN, WIN * WIN, local_width)
    key_flat = key_grad.reshape(NWIN, NWIN, WIN * WIN, local_width)
    value_flat = value_grad.reshape(NWIN, NWIN, WIN * WIN, local_width)
    qv_acc = jnp.stack([jnp.sum(query_flat, axis=(0, 1, 2)), jnp.sum(value_flat, axis=(0, 1, 2))])
    stacked = jnp.stack([query_flat, key_flat, value_flat]).astype(jnp.bfloat16)
    qkv_acc = jnp.einsum("abpd,sabpc->sdc", windows, stacked, preferred_element_type=jnp.float32)
    normed_back = jnp.einsum(
        "sabpc,sdc->abpd", stacked, qkv_full, preferred_element_type=jnp.float32
    )
    first_grad = lax.psum_scatter(
        from_windows(normed_back).astype(jnp.bfloat16), "tensor", scatter_dimension=0, tiled=True
    ).astype(jnp.float32)
    first_value, first_back = jax.vjp(layer_norm, source, gains_wide[0], shifts_wide[0])
    source_part, first_gain, first_shift = first_back(first_grad)
    gain_acc = jnp.stack([first_gain, second_gain])
    shift_acc = jnp.stack([first_shift, second_shift])
    input_grads = [middle_grad + source_part]
    qkv_grad, proj_grad, up_grad, down_grad = (
        lax.psum_scatter(
            qkv_acc.astype(jnp.bfloat16), "dp", scatter_dimension=1, tiled=True
        ).astype(jnp.float32),
        lax.psum_scatter(
            proj_acc.astype(jnp.bfloat16), "dp", scatter_dimension=1, tiled=True
        ).astype(jnp.float32),
        lax.psum_scatter(up_acc.astype(jnp.bfloat16), "dp", scatter_dimension=0, tiled=True).astype(
            jnp.float32
        ),
        lax.psum_scatter(
            down_acc.astype(jnp.bfloat16), "dp", scatter_dimension=1, tiled=True
        ).astype(jnp.float32),
    )
    qv_grad, up_bias_grad = lax.psum((qv_acc, up_bias_acc), "dp")
    gains_grad, shifts_grad, out_grad, table_grad, loss_sum = lax.psum(
        (gain_acc, shift_acc, out_bias_acc, table_acc, loss_total), ("dp", "tensor")
    )
    element_count = images * row_count * GRID * D * lax.axis_size("dp") * lax.axis_size("tensor")
    loss = loss_sum / element_count
    return (
        jnp.stack(outputs),
        jnp.stack(input_grads),
        loss,
        qkv_grad,
        proj_grad,
        up_grad,
        down_grad,
        qv_grad,
        up_bias_grad,
        gains_grad,
        shifts_grad,
        out_grad,
        table_grad,
    )


def solution(mesh):
    in_specs = (
        P("dp", "tensor", None, None),
        P("dp", "tensor", None, None),
        P("dp", "tensor", None, None),
        P(None, "dp", "tensor"),
        P("tensor", "dp"),
        P("dp", "tensor"),
        P("tensor", "dp"),
        P(None, "tensor"),
        P("tensor"),
        P(),
        P(),
        P(),
        P(),
    )
    out_specs = (
        P("dp", "tensor", None, None),
        P("dp", "tensor", None, None),
        P(),
        P(None, "dp", "tensor"),
        P("tensor", "dp"),
        P("dp", "tensor"),
        P("tensor", "dp"),
        P(None, "tensor"),
        P("tensor"),
        P(),
        P(),
        P(),
        P(),
    )
    return jax.shard_map(shards, mesh=mesh, in_specs=in_specs, out_specs=out_specs, check_vma=False)
```

profile of v0, /device:TPU:0, one launch (start us, length us, event | category | flops | bytes accessed | tf_op | source)
XLA Modules:
  0.0 2018.4 jit_solution(13288147670114072156)
XLA Ops:
  18.5 36.7 %all_gather.26 = bf16[320,1280]{0,1:T(8,128)(2,1)} all-gather(bf16[320,160]{0,1:T(8,128)(2,1)S(1)} %copy-done.44), channel_id=1, replica_groups=mesh['dp'=8,'tensor'=4] {'dp'}, dimensions={1}, use_global_device_ids=true | all-gather | bytes 921600 | tf_op jit(solution)/shard_map/all_gather | solution.py:145
  55.2 34.5 %all-gather.8.cloned.1.call-done = bf16[64,64,1280]{2,1,0:T(8,128)(2,1)} async-done(((bf16[16,64,1280]{2,1,0:T(8,128)(2,1)}), bf16[64,64,1280]{2,1,0:T(8,128)(2,1)}) %all-gather.8.cloned.1.call-update) | async-done | bytes 10485776 | tf_op jit(solution)/shard_map/all_gather | solution.py:160
  131.9 19.4 reshape.319
  151.3 24.5 %fusion.109 = f32[3,5,5,196,320]{4,3,0,2,1:T(8,128)} fusion(bf16[5,5,196,1280,1]{3,2,1,0,4:T(8,128)(2,1)} %reshape.319, bf16[3,1280,320]{2,1,0:T(8,128)(2,1)} %all-gather.10.cloned.1.call-done), kind=kOutput, calls=%fused_computation.142 | convolution fusion | flops 12042240000 | bytes 33817600 | tf_op jit(solution)/shard_map/abpd,sdc->sabpc/dot_general | solution.py:162
  231.1 193.3 %while.31 = (s32[]{:T(128)}, bf16[5,5,196,4,80]{2,4,3,1,0:T(8,128)(2,1)}, f32[5,5,4,196]{3,2,1,0:T(4,128)}, bf16[5,5,196,4,80]{2,4,3,1,0:T(8,128)(2,1)}, bf16[5,...) while((s32[]{:T(128)}, ...), condition=%wide.region_5.6_spmd.clone, body=%wide.region_2.5_spmd.clone.sunk | while | flops 322814336 | bytes 44160668 | solution.py:166
  470.1 84.2 %reduce-scatter.11.cloned.1.call-done = bf16[16,64,1280]{2,1,0:T(8,128)(2,1)} async-done(((bf16[64,64,1280]{2,1,0:T(8,128)(2,1)}), bf16[16,64,1280]{2,1,0:T(8,128)(2,1)}) %reduce-scatter.11.cloned.1.call-update) | async-done | bytes 2621456 | tf_op jit(solution)/shard_map/reduce_scatter | solution.py:171
  562.9 55.4 %all-gather.14.cloned.1.call-done = bf16[1280,1280]{1,0:T(8,128)(2,1)} async-done(((bf16[160,1280]{1,0:T(8,128)(2,1)}), bf16[1280,1280]{1,0:T(8,128)(2,1)}) %all-gather.14.cloned.1.call-update) | async-done | bytes 3276816 | tf_op jit(solution)/shard_map/all_gather | solution.py:146
  618.3 70.8 %all-gather.12.cloned.1.call-done = bf16[64,64,1280]{2,1,0:T(8,128)(2,1)} async-done(((bf16[16,64,1280]{2,1,0:T(8,128)(2,1)}), bf16[64,64,1280]{2,1,0:T(8,128)(2,1)}) %all-gather.12.cloned.1.call-update) | async-done | bytes 10485776 | tf_op jit(solution)/shard_map/all_gather | solution.py:181
  689.1 60.9 %multiply_convert_fusion = (bf16[64,64,1280]{2,1,0:T(8,128)(2,1)}, f32[64,64,1280]{2,1,0:T(8,128)}, f32[64,64,1280]{2,1,0:T(8,128)}) fusion(f32[1280]{0:T(1024)S(1)} %convert_element_type.209, bf16[64,64,1280]{2,1,0:T(8,128)(2,1)} %all-gather.12.cloned.1.call-done, bf16[1280,1280]{1,0:T(8,128)(2,1)} %all-gather.14.cloned.1.call-done), kind=kOutput, calls=%fused_computation.117 | convolution fusion | flops 13767802880 | bytes 66196480 | tf_op jit(solution)/shard_map/xyd,dm->xym/dot_general | solution.py:183
  753.2 20.1 convolution_convert_fusion.1
  773.4 84.0 %reduce-scatter.13.cloned.1.call-done = bf16[16,64,1280]{2,1,0:T(8,128)(2,1)} async-done(((bf16[64,64,1280]{2,1,0:T(8,128)(2,1)}), bf16[16,64,1280]{2,1,0:T(8,128)(2,1)}) %reduce-scatter.13.cloned.1.call-update) | async-done | bytes 2621456 | tf_op jit(solution)/shard_map/reduce_scatter | solution.py:188
  868.4 70.3 %all-gather.18.cloned.1.call-done = bf16[64,64,1280]{2,1,0:T(8,128)(2,1)} async-done(((bf16[16,64,1280]{2,1,0:T(8,128)(2,1)}), bf16[64,64,1280]{2,1,0:T(8,128)(2,1)}) %all-gather.18.cloned.1.call-update) | async-done | bytes 10485776 | tf_op jit(solution)/shard_map/all_gather | solution.py:202
  938.7 30.7 %fusion.169 = (f32[1280]{0:T(1024)}, bf16[64,64,1280]{2,1,0:T(8,128)(2,1)}) fusion(f32[64,64,1280]{2,1,0:T(8,128)} %get-tuple-element.416, f32[64,64,1280]{2,1,0:T(8,128)} %get-tuple-element.430, bf16[64,64,1280]{2,1,0:T(8,128)(2,1)} %all-gather.18.cloned.1.call-done, bf16[1280,1280]{0,1:T(8,128)(2,1)} %all-gather.16.cloned.1.call-done), kind=kOutput, calls=%fused_computation.252 | convolution fusion | flops 13500414976 | bytes 66196480 | tf_op jit(solution)/shard_map/xyd,md->xym/dot_general | solution.py:204
  969.4 19.9 convolution_convert_fusion
  989.4 85.4 %reduce-scatter.15.cloned.1.call-done = bf16[16,64,1280]{2,1,0:T(8,128)(2,1)} async-done(((bf16[64,64,1280]{2,1,0:T(8,128)(2,1)}), bf16[16,64,1280]{2,1,0:T(8,128)(2,1)}) %reduce-scatter.15.cloned.1.call-update) | async-done | bytes 2621456 | tf_op jit(solution)/shard_map/reduce_scatter | solution.py:213
  1096.3 20.8 %fusion.112 = bf16[1280,1280]{0,1:T(8,128)(2,1)} fusion(bf16[64,64,1280]{2,1,0:T(8,128)(2,1)} %get-tuple-element.415, bf16[64,64,1280]{2,1,0:T(8,128)(2,1)} %all-gather.18.cloned.1.call-done), kind=kOutput, calls=%fused_computation.156 | convolution fusion | flops 13423411200 | bytes 24248320 | tf_op jit(solution)/shard_map/xym,xyd->md/dot_general | solution.py:203
  1117.2 21.1 %fusion.113 = bf16[1280,1280]{1,0:T(8,128)(2,1)} fusion(bf16[64,64,1280]{2,1,0:T(8,128)(2,1)} %all-gather.12.cloned.1.call-done, bf16[64,64,1280]{2,1,0:T(8,128)(2,1)} %get-tuple-element.432), kind=kOutput, calls=%fused_computation.157 | convolution fusion | flops 13423411200 | bytes 24248320 | tf_op jit(solution)/shard_map/xyd,xym->dm/dot_general | solution.py:211
  1138.4 28.2 %all-gather.20.cloned.1.call-done = bf16[64,64,1280]{2,1,0:T(8,128)(2,1)} async-done(((bf16[16,64,1280]{2,1,0:T(8,128)(2,1)}), bf16[64,64,1280]{2,1,0:T(8,128)(2,1)}) %all-gather.20.cloned.1.call-update) | async-done | bytes 10485776 | tf_op jit(solution)/shard_map/all_gather | solution.py:226
  1211.2 468.2 %while.32 = (s32[]{:T(128)}, f32[5,5,196,4,80]{2,4,3,1,0:T(8,128)}, bf16[5,5,196,4,80]{2,4,3,1,0:T(8,128)(2,1)}, f32[5,5,196,4,80]{2,4,3,1,0:T(8,128)}, f32[5,2,...) while((s32[]{:T(128)}, f32[5,5,196,4,80]{2,4,3,1,0:T(8,128)}, ...), condition=%wide.region_17.18_spmd.clone.clone, body=%wide.region_13.17_spmd.clone.clone.sunk | while | flops 1137800704 | bytes 142737584 | solution.py:234
  1763.5 25.8 %bitcast_convert_fusion = bf16[5,5,196,1280]{3,2,1,0:T(8,128)(2,1)} fusion(bf16[1,5,5,196,320]{4,3,0,2,1:T(8,128)(2,1)} %copy.127, bf16[1,5,5,196,320]{4,3,0,2,1:T(8,128)(2,1)} %copy.126, bf16[1,5,5,196,320]{4,3,0,2,1:T(8,128)(2,1)} %copy.125, bf16[3,1280,320]{2,1,0:T(8,128)(2,1)} %all-gather.10.cloned.1.call-done), kind=kOutput, calls=%fused_computation.114 | convolution fusion | flops 12057920512 | bytes 24409600 | tf_op jit(solution)/shard_map/sabpc,sdc->abpd/dot_general | solution.py:245
  1789.3 19.4 reshape.299
  1854.8 37.5 %all-reduce.3 = (f32[2,320]{1,0:T(2,128)}, f32[1280]{0:T(1024)}) all-reduce(f32[2,320]{1,0:T(2,128)S(1)} %pad_maximum_fusion.10, f32[1280]{0:T(1024)S(1)} %copy-done.57), channel_id=1, replica_groups=mesh['dp'=8,'tensor'=4] {'dp'}, use_global_device_ids=true, to_apply=%region_29.30 | all-reduce | flops 1920 | bytes 15360 | tf_op jit(solution)/shard_map/psum | solution.py:270
  1898.7 56.9 %reduce-scatter.17.cloned.1.call-done = bf16[16,64,1280]{2,1,0:T(8,128)(2,1)} async-done(((bf16[64,64,1280]{2,1,0:T(8,128)(2,1)}), bf16[16,64,1280]{2,1,0:T(8,128)(2,1)}) %reduce-scatter.17.cloned.1.call-update) | async-done | bytes 2621456 | tf_op jit(solution)/shard_map/reduce_scatter | solution.py:248
  1962.5 41.0 %all-reduce.2 = (f32[]{:T(128)}, f32[2,1280]{1,0:T(2,128)}, f32[2,1280]{1,0:T(2,128)}, f32[2,1280]{1,0:T(2,128)}, f32[2,27,80]{2,1,0:T(8,128)S(1)}) all-reduce(f32[]{:T(128)} %get-tuple-element.343, f32[2,1280]{1,0:T(2,128)S(1)} %pad_maximum_fusion.7, ...), channel_id=1, replica_groups=mesh['dp'=8,'tensor'=4] {'dp','tensor'}, use_global_device_ids=true, to_apply=%region_22.23 | all-reduce | flops 12001 | bytes 96008 | tf_op jit(solution)/shard_map/psum | solution.py:271
  (563 shorter events, 1044.1 us)
Async XLA Ops:
  7.2 82.5 %all-gather.8.cloned.1.call-start = ((), (), s32[]{:S(2)}) async-start(), calls=%async_computation.8 | async-start | bytes 13107200 | tf_op jit(solution)/shard_map/all_gather | solution.py:160
  16.7 134.6 %all-gather.10.cloned.1.call-start = ((), (), s32[]{:S(2)}) async-start(), calls=%async_computation.9 | async-start | bytes 3317760 | tf_op jit(solution)/shard_map/all_gather | solution.py:144
  17.4 536.9 %reduce-scatter.11.cloned.1.call-start = ((), (), s32[]{:S(2)}) async-start(), calls=%async_computation.10 | async-start | bytes 13107200 | tf_op jit(solution)/shard_map/reduce_scatter | solution.py:171
  468.8 85.6 %copy-start.5 = (bf16[1,16,64,1280]{3,2,1,0:T(8,128)(2,1)S(1)}, bf16[1,16,64,1280]{3,2,1,0:T(8,128)(2,1)}, u32[]{:S(2)}) copy-start(bf16[1,16,64,1280]{3,2,1,0:T(8,128)(2,1)} %param.17) | copy-start | bytes 7864324
  468.8 149.6 %all-gather.14.cloned.1.call-start = ((), (), s32[]{:S(2)}) async-start(), calls=%async_computation.12 | async-start | bytes 3686400 | tf_op jit(solution)/shard_map/all_gather | solution.py:146
  469.4 219.8 %all-gather.12.cloned.1.call-start = ((), (), s32[]{:S(2)}) async-start(), calls=%async_computation.11 | async-start | bytes 13107200 | tf_op jit(solution)/shard_map/all_gather | solution.py:181
  470.1 89.0 %copy-start.30 = (f32[1280]{0:T(1024)}, f32[1280]{0:T(1024)S(1)}, u32[]{:S(2)}) copy-start(f32[1280]{0:T(1024)S(1)} %get-tuple-element.352) | copy-start | bytes 15364
  562.3 190.9 %all-gather.16.cloned.1.call-start = ((), (), s32[]{:S(2)}) async-start(), calls=%async_computation.13 | async-start | bytes 3686400 | tf_op jit(solution)/shard_map/all_gather | solution.py:147
  562.9 294.5 %reduce-scatter.13.cloned.1.call-start = ((), (), s32[]{:S(2)}) async-start(), calls=%async_computation.14 | async-start | bytes 13107200 | tf_op jit(solution)/shard_map/reduce_scatter | solution.py:188
  773.3 165.4 %all-gather.18.cloned.1.call-start = ((), (), s32[]{:S(2)}) async-start(), calls=%async_computation.15 | async-start | bytes 13107200 | tf_op jit(solution)/shard_map/all_gather | solution.py:202
  868.3 206.5 %reduce-scatter.15.cloned.1.call-start = ((), (), s32[]{:S(2)}) async-start(), calls=%async_computation.16 | async-start | bytes 13107200 | tf_op jit(solution)/shard_map/reduce_scatter | solution.py:213
  989.3 90.7 %copy-start.49 = (f32[16,64]{1,0:T(8,128)S(1)}, f32[16,64]{1,0:T(8,128)}, u32[]{:S(2)}) copy-start(f32[16,64]{1,0:T(8,128)} %copy-done.48) | copy-start | bytes 12292
  989.4 90.7 %copy-start.43 = (f32[16,64]{1,0:T(8,128)S(1)}, f32[16,64]{1,0:T(8,128)}, u32[]{:S(2)}) copy-start(f32[16,64]{1,0:T(8,128)} %copy-done.42) | copy-start | bytes 12292
  989.4 177.2 %all-gather.20.cloned.1.call-start = ((), (), s32[]{:S(2)}) async-start(), calls=%async_computation.17 | async-start | bytes 13107200 | tf_op jit(solution)/shard_map/all_gather | solution.py:226
  1096.2 754.0 %reduce-scatter.23.cloned.1.call-start = ((), (), s32[]{:S(2)}) async-start(), calls=%async_computation.21 | async-start | bytes 3686400 | tf_op jit(solution)/shard_map/reduce_scatter | solution.py:266
  1117.1 735.3 %reduce-scatter.21.cloned.1.call-start = ((), (), s32[]{:S(2)}) async-start(), calls=%async_computation.20 | async-start | bytes 3686400 | tf_op jit(solution)/shard_map/reduce_scatter | solution.py:263
  1138.4 753.9 %reduce-scatter.19.cloned.1.call-start = ((), (), s32[]{:S(2)}) async-start(), calls=%async_computation.19 | async-start | bytes 1105920 | tf_op jit(solution)/shard_map/reduce_scatter | solution.py:260
  1731.3 162.5 %reduce-scatter.25.cloned.1.call-start = ((), (), s32[]{:S(2)}) async-start(), calls=%async_computation.22 | async-start | bytes 2949120
  1763.4 192.2 %reduce-scatter.17.cloned.1.call-start = ((), (), s32[]{:S(2)}) async-start(), calls=%async_computation.18 | async-start | bytes 13107200 | tf_op jit(solution)/shard_map/reduce_scatter | solution.py:248
  1849.6 106.0 %copy-start.7 = (bf16[1,16,64,1280]{3,2,1,0:T(8,128)(2,1)S(1)}, bf16[1,16,64,1280]{3,2,1,0:T(8,128)(2,1)}, u32[]{:S(2)}) copy-start(bf16[1,16,64,1280]{3,2,1,0:T(8,128)(2,1)} %param.17) | copy-start | bytes 7864324
  1849.6 106.0 %copy-start.33 = (f32[16,64]{1,0:T(8,128)S(1)}, f32[16,64]{1,0:T(8,128)}, u32[]{:S(2)}) copy-start(f32[16,64]{1,0:T(8,128)} %copy-done.32) | copy-start | bytes 12292
  1849.6 106.0 %copy-start.37 = (f32[1280]{0:T(1024)S(1)}, f32[1280]{0:T(1024)}, u32[]{:S(2)}) copy-start(f32[1280]{0:T(1024)} %copy-done.36) | copy-start | bytes 15364
  1852.4 107.0 %copy-start.47 = (f32[16,64]{1,0:T(8,128)S(1)}, f32[16,64]{1,0:T(8,128)}, u32[]{:S(2)}) copy-start(f32[16,64]{1,0:T(8,128)} %copy-done.46) | copy-start | bytes 12292
  1852.4 107.1 %copy-start.41 = (f32[16,64]{1,0:T(8,128)S(1)}, f32[16,64]{1,0:T(8,128)}, u32[]{:S(2)}) copy-start(f32[16,64]{1,0:T(8,128)} %copy-done.40) | copy-start | bytes 12292
  (99 other events, 999.7 us)
Sparse Core Ops, SparseCore 0:
  16.8 72.8 all-gather.7
  91.9 58.3 all-gather.9
  468.9 85.3 reduce-scatter.10
  556.3 61.9 all-gather.13
  620.3 68.7 all-gather.11
  691.2 61.9 all-gather.15
  773.4 83.8 reduce-scatter.12
  868.5 70.1 all-gather.17
  989.5 85.2 reduce-scatter.14
  1096.4 70.1 all-gather.19
  1170.2 76.0 reduce-scatter.22
  1250.2 74.9 reduce-scatter.20
  1731.5 63.6 reduce-scatter.18
  1798.9 69.6 reduce-scatter.24
  1871.2 84.3 reduce-scatter.16
where the time goes:
time: 2030 us; the launch traced here: 2020 us
  matrix products  677 us (33%)
  waiting for transfers between devices  575 us (28%)
  local copies, waits for them, and re-layouts  520 us (26%)
  blocking collectives  115 us (6%)
  other arithmetic  105 us (5%)
    reduce_scatter x1, waiting for transfers between devices, shards(): lax.psum_scatter(jnp.einsum('xym,dm->xyd', row_piece, up_matrix, preferre...  85.4 us
    reduce_scatter x1, waiting for transfers between devices, shards(): lax.psum_scatter(jnp.einsum('xyc,cd->xyd', row_piece, proj_full, preferre...  84.2 us
    reduce_scatter x1, waiting for transfers between devices, shards(): lax.psum_scatter(jnp.einsum('xym,md->xyd', row_piece, down_matrix, prefer...  84 us
    dot_general x10, matrix products, score_block(): jnp.einsum('wqhr,qkr->whqk', along_wide, wide_sel, precision=highest)  78 us
    dot_general x10, matrix products, score_block(): jnp.einsum('wqhr,qkr->whqk', along_high, high_sel, precision=highest)  77.8 us
    all_gather x1, waiting for transfers between devices, shards(): mlp_input = lax.all_gather(normed_two, 'tensor', axis=0, tiled=True)  70.8 us
    all_gather x1, waiting for transfers between devices, shards(): grad_rows = lax.all_gather(result_low, 'tensor', axis=0, tiled=True)  70.3 us
    dot_general x1, matrix products, shards(): jnp.einsum('xyd,dm->xym', mlp_input, up_matrix, preferred_element_type=jn...  60.9 us
  transfers between devices with their start and end apart: 15, of which 10 were waited for; matrix products, arithmetic and copies ran while one was open for 42% of the time, Pallas kernels for 0%

commit v1 on v0

--- a/solution.py
+++ b/solution.py
@@ -178,7 +178,15 @@
     ).astype(jnp.float32)
     middle = source + attn_branch + out_biases[0].astype(jnp.float32)
     normed_two = layer_norm(middle, gains_wide[1], shifts_wide[1]).astype(jnp.bfloat16)
-    mlp_input = lax.all_gather(normed_two, "tensor", axis=0, tiled=True)
+    ways, here = (lax.axis_size("tensor"), lax.axis_index("tensor"))
+    grown, reach = (normed_two, 1)
+    while reach < ways:
+        theirs = lax.ppermute(grown, "tensor", [(d, d ^ reach) for d in range(ways)])
+        mine_first = jnp.concatenate([grown, theirs], axis=0)
+        theirs_first = jnp.concatenate([theirs, grown], axis=0)
+        grown = jnp.where(here & reach == 0, mine_first, theirs_first)
+        reach = 2 * reach
+    mlp_input = grown
     hidden = (
         jnp.einsum("xyd,dm->xym", mlp_input, up_matrix, preferred_element_type=jnp.float32)
         + up_bias_all

time: 2030 us -> 2030 us (level)
    all_gather x1 -> x0, waiting for transfers between devices: 70.8 us -> none  [shards(): mlp_input = lax.all_gather(normed_two, 'tensor', axis=0, tiled=True)]
    ppermute x0 -> x2, waiting for transfers between devices: none -> 68.9 us  [shards(): lax.ppermute(grown, 'tensor', [(d, d ^ reach) for d in range(ways)])]
  transfers between devices with their start and end apart: 15 -> 16, of which waited for: 10 -> 10; matrix products, arithmetic and copies ran while one was open for 42% -> 42% of each run, Pallas kernels for 0% -> 0%
where the time goes in v1:
time: 2030 us; the launch traced here: 2020 us
  matrix products  685 us (34%)
  waiting for transfers between devices  564 us (28%)
  local copies, waits for them, and re-layouts  518 us (26%)
  blocking collectives  115 us (6%)
  other arithmetic  110 us (5%)
    reduce_scatter x1, waiting for transfers between devices, shards(): lax.psum_scatter(jnp.einsum('xym,md->xyd', row_piece, down_matrix, prefer...  85.4 us
    reduce_scatter x1, waiting for transfers between devices, shards(): lax.psum_scatter(jnp.einsum('xym,dm->xyd', row_piece, up_matrix, preferre...  85.4 us
    reduce_scatter x1, waiting for transfers between devices, shards(): lax.psum_scatter(jnp.einsum('xyc,cd->xyd', row_piece, proj_full, preferre...  84.2 us
    dot_general x10, matrix products, score_block(): jnp.einsum('wqhr,qkr->whqk', along_high, high_sel, precision=highest)  77.4 us
    dot_general x10, matrix products, score_block(): jnp.einsum('wqhr,qkr->whqk', along_wide, wide_sel, precision=highest)  77.3 us
    all_gather x1, waiting for transfers between devices, shards(): grad_rows = lax.all_gather(result_low, 'tensor', axis=0, tiled=True)  70.3 us
    ppermute x2, waiting for transfers between devices, shards(): lax.ppermute(grown, 'tensor', [(d, d ^ reach) for d in range(ways)])  68.9 us
    dot_general x1, matrix products, shards(): jnp.einsum('xyd,dm->xym', mlp_input, up_matrix, preferred_element_type=jn...  68.6 us
  transfers between devices with their start and end apart: 16, of which 10 were waited for; matrix products, arithmetic and copies ran while one was open for 42% of the time, Pallas kernels for 0%

profile of v1, /device:TPU:0, one launch (start us, length us, event | category | flops | bytes accessed | tf_op | source)
XLA Modules:
  0.0 2020.8 jit_solution(8673895277755603607)
XLA Ops:
  18.5 36.7 %all_gather.23 = bf16[320,1280]{0,1:T(8,128)(2,1)} all-gather(bf16[320,160]{0,1:T(8,128)(2,1)S(1)} %copy-done.44), channel_id=1, replica_groups=mesh['dp'=8,'tensor'=4] {'dp'}, dimensions={1}, use_global_device_ids=true | all-gather | bytes 921600 | tf_op jit(solution)/shard_map/all_gather | solution.py:145
  55.2 34.5 %all-gather.7.cloned.1.call-done = bf16[64,64,1280]{2,1,0:T(8,128)(2,1)} async-done(((bf16[16,64,1280]{2,1,0:T(8,128)(2,1)}), bf16[64,64,1280]{2,1,0:T(8,128)(2,1)}) %all-gather.7.cloned.1.call-update) | async-done | bytes 10485776 | tf_op jit(solution)/shard_map/all_gather | solution.py:160
  131.9 19.4 reshape.319
  151.4 24.6 %fusion.109 = f32[3,5,5,196,320]{4,3,0,2,1:T(8,128)} fusion(bf16[5,5,196,1280,1]{3,2,1,0,4:T(8,128)(2,1)} %reshape.319, bf16[3,1280,320]{2,1,0:T(8,128)(2,1)} %all-gather.9.cloned.1.call-done), kind=kOutput, calls=%fused_computation.143 | convolution fusion | flops 12042240000 | bytes 33817600 | tf_op jit(solution)/shard_map/abpd,sdc->sabpc/dot_general | solution.py:162
  231.4 193.3 %while.31 = (s32[]{:T(128)}, bf16[5,5,196,4,80]{2,4,3,1,0:T(8,128)(2,1)}, f32[5,5,4,196]{3,2,1,0:T(4,128)}, bf16[5,5,196,4,80]{2,4,3,1,0:T(8,128)(2,1)}, bf16[5,...) while((s32[]{:T(128)}, ...), condition=%wide.region_5.6_spmd.clone, body=%wide.region_2.5_spmd.clone.sunk | while | flops 322814336 | bytes 44160668 | solution.py:166
  470.4 84.2 %reduce-scatter.11.cloned.1.call-done = bf16[16,64,1280]{2,1,0:T(8,128)(2,1)} async-done(((bf16[64,64,1280]{2,1,0:T(8,128)(2,1)}), bf16[16,64,1280]{2,1,0:T(8,128)(2,1)}) %reduce-scatter.11.cloned.1.call-update) | async-done | bytes 2621456 | tf_op jit(solution)/shard_map/reduce_scatter | solution.py:171
  572.6 51.1 %all-gather.11.cloned.1.call-done = bf16[1280,1280]{1,0:T(8,128)(2,1)} async-done(((bf16[160,1280]{1,0:T(8,128)(2,1)}), bf16[1280,1280]{1,0:T(8,128)(2,1)}) %all-gather.11.cloned.1.call-update) | async-done | bytes 3276816 | tf_op jit(solution)/shard_map/all_gather | solution.py:146
  623.7 63.9 %collective-permute-done.1 = bf16[32,64,1280]{2,1,0:T(8,128)(2,1)} collective-permute-done((bf16[32,64,1280]{2,1,0:T(8,128)(2,1)}, bf16[32,64,1280]{2,1,0:T(8,128)(2,1)}, u32[]{:S(2)}, u32[]{:S(2)}) %collective-permute-start.1) | collective-permute-done | bytes 5242912 | tf_op jit(solution)/shard_map/ppermute | solution.py:184
  687.6 68.6 %multiply_convert_fusion = (bf16[64,64,1280]{2,1,0:T(8,128)(2,1)}, f32[64,64,1280]{2,1,0:T(8,128)}, f32[64,64,1280]{2,1,0:T(8,128)}) fusion(f32[1280]{0:T(1024)S(1)} %convert_element_type.209, bf16[1280,1280]{1,0:T(8,128)(2,1)} %all-gather.11.cloned.1.call-done, bf16[32,64,1280]{2,1,0:T(8,128)(2,1)} %collective-permute-done.1, ...), kind=kOutput, calls=%fused_computation.117 | convolution fusion | flops 13783531520 | bytes 66196480 | tf_op jit(solution)/shard_map/xyd,dm->xym/dot_general | solution.py:191
  756.2 20.2 %convolution_convert_fusion.1 = bf16[64,64,1280]{2,1,0:T(8,128)(2,1)} fusion(bf16[64,64,1280]{2,1,0:T(8,128)(2,1)} %get-tuple-element.415, bf16[1280,1280]{0,1:T(8,128)(2,1)} %all-gather.13.cloned.1.call-done), kind=kOutput, calls=%fused_computation.135 | convolution fusion | flops 13427015680 | bytes 24248320 | tf_op jit(solution)/shard_map/xym,md->xyd/dot_general | solution.py:197
  776.5 85.4 %reduce-scatter.13.cloned.1.call-done = bf16[16,64,1280]{2,1,0:T(8,128)(2,1)} async-done(((bf16[64,64,1280]{2,1,0:T(8,128)(2,1)}), bf16[16,64,1280]{2,1,0:T(8,128)(2,1)}) %reduce-scatter.13.cloned.1.call-update) | async-done | bytes 2621456 | tf_op jit(solution)/shard_map/reduce_scatter | solution.py:196
  872.9 70.3 %all-gather.15.cloned.1.call-done = bf16[64,64,1280]{2,1,0:T(8,128)(2,1)} async-done(((bf16[16,64,1280]{2,1,0:T(8,128)(2,1)}), bf16[64,64,1280]{2,1,0:T(8,128)(2,1)}) %all-gather.15.cloned.1.call-update) | async-done | bytes 10485776 | tf_op jit(solution)/shard_map/all_gather | solution.py:210
  943.2 30.5 %fusion.171 = (f32[1280]{0:T(1024)}, bf16[64,64,1280]{2,1,0:T(8,128)(2,1)}) fusion(f32[64,64,1280]{2,1,0:T(8,128)} %get-tuple-element.416, f32[64,64,1280]{2,1,0:T(8,128)} %get-tuple-element.430, bf16[64,64,1280]{2,1,0:T(8,128)(2,1)} %all-gather.15.cloned.1.call-done, bf16[1280,1280]{0,1:T(8,128)(2,1)} %all-gather.13.cloned.1.call-done), kind=kOutput, calls=%fused_computation.256 | convolution fusion | flops 13500414976 | bytes 66196480 | tf_op jit(solution)/shard_map/xyd,md->xym/dot_general | solution.py:212
  973.7 19.8 convolution_convert_fusion
  993.6 85.4 %reduce-scatter.15.cloned.1.call-done = bf16[16,64,1280]{2,1,0:T(8,128)(2,1)} async-done(((bf16[64,64,1280]{2,1,0:T(8,128)(2,1)}), bf16[16,64,1280]{2,1,0:T(8,128)(2,1)}) %reduce-scatter.15.cloned.1.call-update) | async-done | bytes 2621456 | tf_op jit(solution)/shard_map/reduce_scatter | solution.py:221
  1100.7 20.8 %fusion.112 = bf16[1280,1280]{0,1:T(8,128)(2,1)} fusion(bf16[64,64,1280]{2,1,0:T(8,128)(2,1)} %get-tuple-element.415, bf16[64,64,1280]{2,1,0:T(8,128)(2,1)} %all-gather.15.cloned.1.call-done), kind=kOutput, calls=%fused_computation.157 | convolution fusion | flops 13423411200 | bytes 24248320 | tf_op jit(solution)/shard_map/xym,xyd->md/dot_general | solution.py:211
  1121.6 23.0 %fusion.113 = bf16[1280,1280]{1,0:T(8,128)(2,1)} fusion(bf16[64,64,1280]{2,1,0:T(8,128)(2,1)} %get-tuple-element.432, bf16[32,64,1280]{2,1,0:T(8,128)(2,1)} %collective-permute-done.1, bf16[32,64,1280]{2,1,0:T(8,128)(2,1)} %maximum_select_fusion.1, pred[]{:T(512)S(6)} %eq.64), kind=kOutput, calls=%fused_computation.158 | convolution fusion | flops 13439139840 | bytes 24248320 | tf_op jit(solution)/shard_map/xyd,xym->dm/dot_general | solution.py:219
  1144.7 26.3 %all-gather.17.cloned.1.call-done = bf16[64,64,1280]{2,1,0:T(8,128)(2,1)} async-done(((bf16[16,64,1280]{2,1,0:T(8,128)(2,1)}), bf16[64,64,1280]{2,1,0:T(8,128)(2,1)}) %all-gather.17.cloned.1.call-update) | async-done | bytes 10485776 | tf_op jit(solution)/shard_map/all_gather | solution.py:234
  1215.7 466.2 %while.32 = (s32[]{:T(128)}, f32[5,5,196,4,80]{2,4,3,1,0:T(8,128)}, bf16[5,5,196,4,80]{2,4,3,1,0:T(8,128)(2,1)}, f32[5,5,196,4,80]{2,4,3,1,0:T(8,128)}, f32[5,2,...) while((s32[]{:T(128)}, f32[5,5,196,4,80]{2,4,3,1,0:T(8,128)}, ...), condition=%wide.region_17.18_spmd.clone.clone, body=%wide.region_13.17_spmd.clone.clone.sunk | while | flops 1137800704 | bytes 142737584 | solution.py:242
  1765.6 25.6 %bitcast_convert_fusion = bf16[5,5,196,1280]{3,2,1,0:T(8,128)(2,1)} fusion(bf16[1,5,5,196,320]{4,3,0,2,1:T(8,128)(2,1)} %copy.127, bf16[1,5,5,196,320]{4,3,0,2,1:T(8,128)(2,1)} %copy.126, bf16[1,5,5,196,320]{4,3,0,2,1:T(8,128)(2,1)} %copy.125, bf16[3,1280,320]{2,1,0:T(8,128)(2,1)} %all-gather.9.cloned.1.call-done), kind=kOutput, calls=%fused_computation.114 | convolution fusion | flops 12057920512 | bytes 24409600 | tf_op jit(solution)/shard_map/sabpc,sdc->abpd/dot_general | solution.py:253
  1791.2 19.4 reshape.299
  1856.7 37.6 %all-reduce.3 = (f32[2,320]{1,0:T(2,128)}, f32[1280]{0:T(1024)}) all-reduce(f32[2,320]{1,0:T(2,128)S(1)} %pad_maximum_fusion.10, f32[1280]{0:T(1024)S(1)} %copy-done.57), channel_id=1, replica_groups=mesh['dp'=8,'tensor'=4] {'dp'}, use_global_device_ids=true, to_apply=%region_29.30 | all-reduce | flops 1920 | bytes 15360 | tf_op jit(solution)/shard_map/psum | solution.py:278
  1900.7 57.2 %reduce-scatter.17.cloned.1.call-done = bf16[16,64,1280]{2,1,0:T(8,128)(2,1)} async-done(((bf16[64,64,1280]{2,1,0:T(8,128)(2,1)}), bf16[16,64,1280]{2,1,0:T(8,128)(2,1)}) %reduce-scatter.17.cloned.1.call-update) | async-done | bytes 2621456 | tf_op jit(solution)/shard_map/reduce_scatter | solution.py:256
  1964.9 41.0 %all-reduce.2 = (f32[]{:T(128)}, f32[2,1280]{1,0:T(2,128)}, f32[2,1280]{1,0:T(2,128)}, f32[2,1280]{1,0:T(2,128)}, f32[2,27,80]{2,1,0:T(8,128)S(1)}) all-reduce(f32[]{:T(128)} %get-tuple-element.343, f32[2,1280]{1,0:T(2,128)S(1)} %pad_maximum_fusion.7, ...), channel_id=1, replica_groups=mesh['dp'=8,'tensor'=4] {'dp','tensor'}, use_global_device_ids=true, to_apply=%region_22.23 | all-reduce | flops 12001 | bytes 96008 | tf_op jit(solution)/shard_map/psum | solution.py:279
  (565 shorter events, 1048.1 us)
Async XLA Ops:
  7.2 82.5 %all-gather.7.cloned.1.call-start = ((), (), s32[]{:S(2)}) async-start(), calls=%async_computation.8 | async-start | bytes 13107200 | tf_op jit(solution)/shard_map/all_gather | solution.py:160
  16.6 134.7 %all-gather.9.cloned.1.call-start = ((), (), s32[]{:S(2)}) async-start(), calls=%async_computation.9 | async-start | bytes 3317760 | tf_op jit(solution)/shard_map/all_gather | solution.py:144
  17.4 537.2 %reduce-scatter.11.cloned.1.call-start = ((), (), s32[]{:S(2)}) async-start(), calls=%async_computation.10 | async-start | bytes 13107200 | tf_op jit(solution)/shard_map/reduce_scatter | solution.py:171
  469.1 154.7 %all-gather.11.cloned.1.call-start = ((), (), s32[]{:S(2)}) async-start(), calls=%async_computation.11 | async-start | bytes 3686400 | tf_op jit(solution)/shard_map/all_gather | solution.py:146
  470.4 88.4 %copy-start.30 = (f32[1280]{0:T(1024)}, f32[1280]{0:T(1024)S(1)}, u32[]{:S(2)}) copy-start(f32[1280]{0:T(1024)S(1)} %get-tuple-element.352) | copy-start | bytes 15364
  561.4 5.2 collective-permute-start
  561.5 194.7 %all-gather.13.cloned.1.call-start = ((), (), s32[]{:S(2)}) async-start(), calls=%async_computation.12 | async-start | bytes 3686400 | tf_op jit(solution)/shard_map/all_gather | solution.py:147
  572.2 115.4 %collective-permute-start.1 = (bf16[32,64,1280]{2,1,0:T(8,128)(2,1)}, bf16[32,64,1280]{2,1,0:T(8,128)(2,1)}, u32[]{:S(2)}, u32[]{:S(2)}) collective-permute-start(bf16[32,64,1280]{2,1,0:T(8,128)(2,1)} %maximum_select_fusion.1), channel_id=1, source_target_pairs={{0,2},{1,3},{2,0},{3,1},{4,6},{5,7},{6,4},{7,5},{8,10},{9,11},{10,... | collective-permute-start | bytes 15728648 | tf_op jit(solution)/shard_map/ppermute | solution.py:184
  572.5 289.4 %reduce-scatter.13.cloned.1.call-start = ((), (), s32[]{:S(2)}) async-start(), calls=%async_computation.13 | async-start | bytes 13107200 | tf_op jit(solution)/shard_map/reduce_scatter | solution.py:196
  776.5 166.8 %all-gather.15.cloned.1.call-start = ((), (), s32[]{:S(2)}) async-start(), calls=%async_computation.14 | async-start | bytes 13107200 | tf_op jit(solution)/shard_map/all_gather | solution.py:210
  872.9 206.2 %reduce-scatter.15.cloned.1.call-start = ((), (), s32[]{:S(2)}) async-start(), calls=%async_computation.15 | async-start | bytes 13107200 | tf_op jit(solution)/shard_map/reduce_scatter | solution.py:221
  993.6 90.9 %copy-start.49 = (f32[16,64]{1,0:T(8,128)S(1)}, f32[16,64]{1,0:T(8,128)}, u32[]{:S(2)}) copy-start(f32[16,64]{1,0:T(8,128)} %copy-done.48) | copy-start | bytes 12292
  993.6 90.9 %copy-start.43 = (f32[16,64]{1,0:T(8,128)S(1)}, f32[16,64]{1,0:T(8,128)}, u32[]{:S(2)}) copy-start(f32[16,64]{1,0:T(8,128)} %copy-done.42) | copy-start | bytes 12292
  993.6 177.4 %all-gather.17.cloned.1.call-start = ((), (), s32[]{:S(2)}) async-start(), calls=%async_computation.16 | async-start | bytes 13107200 | tf_op jit(solution)/shard_map/all_gather | solution.py:234
  1100.6 751.7 %reduce-scatter.23.cloned.1.call-start = ((), (), s32[]{:S(2)}) async-start(), calls=%async_computation.20 | async-start | bytes 3686400 | tf_op jit(solution)/shard_map/reduce_scatter | solution.py:274
  1121.5 732.9 %reduce-scatter.21.cloned.1.call-start = ((), (), s32[]{:S(2)}) async-start(), calls=%async_computation.19 | async-start | bytes 3686400 | tf_op jit(solution)/shard_map/reduce_scatter | solution.py:271
  1144.6 749.7 %reduce-scatter.19.cloned.1.call-start = ((), (), s32[]{:S(2)}) async-start(), calls=%async_computation.18 | async-start | bytes 1105920 | tf_op jit(solution)/shard_map/reduce_scatter | solution.py:268
  1733.7 162.2 %reduce-scatter.25.cloned.1.call-start = ((), (), s32[]{:S(2)}) async-start(), calls=%async_computation.21 | async-start | bytes 2949120
  1765.6 192.4 %reduce-scatter.17.cloned.1.call-start = ((), (), s32[]{:S(2)}) async-start(), calls=%async_computation.17 | async-start | bytes 13107200 | tf_op jit(solution)/shard_map/reduce_scatter | solution.py:256
  1851.6 106.3 %copy-start.7 = (bf16[1,16,64,1280]{3,2,1,0:T(8,128)(2,1)S(1)}, bf16[1,16,64,1280]{3,2,1,0:T(8,128)(2,1)}, u32[]{:S(2)}) copy-start(bf16[1,16,64,1280]{3,2,1,0:T(8,128)(2,1)} %param.17) | copy-start | bytes 7864324
  1851.6 106.3 %copy-start.33 = (f32[16,64]{1,0:T(8,128)S(1)}, f32[16,64]{1,0:T(8,128)}, u32[]{:S(2)}) copy-start(f32[16,64]{1,0:T(8,128)} %copy-done.32) | copy-start | bytes 12292
  1851.7 106.3 %copy-start.37 = (f32[1280]{0:T(1024)S(1)}, f32[1280]{0:T(1024)}, u32[]{:S(2)}) copy-start(f32[1280]{0:T(1024)} %copy-done.36) | copy-start | bytes 15364
  1854.4 107.4 %copy-start.47 = (f32[16,64]{1,0:T(8,128)S(1)}, f32[16,64]{1,0:T(8,128)}, u32[]{:S(2)}) copy-start(f32[16,64]{1,0:T(8,128)} %copy-done.46) | copy-start | bytes 12292
  1854.4 107.4 %copy-start.41 = (f32[16,64]{1,0:T(8,128)S(1)}, f32[16,64]{1,0:T(8,128)}, u32[]{:S(2)}) copy-start(f32[16,64]{1,0:T(8,128)} %copy-done.40) | copy-start | bytes 12292
  (100 other events, 1100.7 us)
Sparse Core Ops, SparseCore 0:
  16.8 72.8 all-gather.6
  91.9 58.3 all-gather.8
  469.2 85.3 reduce-scatter.10
  561.6 62.0 all-gather.10
  625.8 60.5 all-gather.12
  776.6 85.3 reduce-scatter.12
  873.0 70.1 all-gather.14
  993.7 85.2 reduce-scatter.14
  1100.7 70.1 all-gather.16
  1174.4 76.0 reduce-scatter.22
  1254.6 75.0 reduce-scatter.20
  1733.8 63.6 reduce-scatter.18
  1801.4 69.5 reduce-scatter.24
  1873.7 84.2 reduce-scatter.16
